TPU v7x, 32 devices: a whole 2x2x4 slice. The times are simulated.
32 devices in a mesh: tm: 4 (over x, core), height: 8 (over z, y).
Axes of the slice: x: 2, y: 2, z: 4, core: 2. Of those that a mesh axis runs over, the one named last changes fastest.
Arguments:
- queries: bfloat16 [16, 64, 4, 1536], P('tm', 'height'), may hold values from -6 to 6
- key_tokens: bfloat16 [16, 64, 4, 1536], P('tm', 'height'), may hold values from -6 to 6
- value_tokens: bfloat16 [16, 64, 4, 1536], P('tm', 'height'), may hold values from -6 to 6
- out_weight: bfloat16 [1536, 3072], P('height'), may hold values from -0.15625 to 0.15625
- out_grad: bfloat16 [16, 64, 4, 3072], P('tm', 'height'), may hold values from -6 to 6
- window_reach: int32 [4, 8, 2], replicated, may hold values from 0 to 2, as said below
- tile_valid: int32 [4, 8], replicated, may hold values 0 or 1
Outputs:
- attn_out: bfloat16 [16, 64, 4, 3072], P('tm', 'height')
- grad_query: bfloat16 [16, 64, 4, 1536], P('tm', 'height')
- grad_key: bfloat16 [16, 64, 4, 1536], P('tm', 'height')
- grad_value: bfloat16 [16, 64, 4, 1536], P('tm', 'height')
- grad_weight: float32 [1536, 3072], P('height', 'tm')
Inputs may be any that keep to these rules, and one draw needn't show every extreme that they name: `window_reach`: entry 0 is a tile's reach in frames and entry 1 its reach in rows; some tile reaches 2 in both.
All inputs are finite; a program needn't handle non-finite values.
Results may differ from a plain program's by a relative error of at most 0.014.
Values may be sent and summed in bfloat16 or wider, within the bound.
A program may use at most 128 MiB of HBM per device.

v0:
```python
import math
import jax
import jax.numpy as jnp
from jax import lax
from jax.sharding import PartitionSpec as P

HEAD_DIM = 128
HALO = 2


def padded(shard, sides, width):
    for axis, dim in sides:
        count, length = (lax.axis_size(axis), shard.shape[dim])
        up = [(i, (i + 1) % count) for i in range(count - 1)]
        down = [(j, i) for i, j in up]
        last = lax.slice_in_dim(shard, length - width, length, axis=dim)
        first = lax.slice_in_dim(shard, 0, width, axis=dim)
        before = lax.ppermute(last, axis, up)
        after = lax.ppermute(first, axis, down)
        shard = jnp.concatenate([before, shard, after], axis=dim)
    return shard


def passed_along(value, axis, steps):
    count = lax.axis_size(axis)
    first, last = (max(0, -steps), min(count, count - steps))
    return lax.ppermute(value, axis, [(source, source + steps) for source in range(first, last)])


def key_mask(
    window_reach, tile_valid, frame_tile, row_tile, tile_frames, tile_rows, margin, columns
):
    tiles_frames = tile_valid.shape[0]
    tiles_rows = tile_valid.shape[1]
    ext_frames = tile_frames + 2 * margin
    ext_rows = tile_rows + 2 * margin
    frame_pos = jnp.arange(ext_frames, dtype=jnp.int32)
    row_pos = jnp.arange(ext_rows, dtype=jnp.int32)
    frame_ids = jnp.arange(tiles_frames, dtype=jnp.int32)
    row_ids = jnp.arange(tiles_rows, dtype=jnp.int32)
    marked = (frame_ids[:, None] == frame_tile) & (row_ids[None, :] == row_tile)
    reach_frame = jnp.sum(jnp.where(marked, window_reach[:, :, 0], 0))
    reach_row = jnp.sum(jnp.where(marked, window_reach[:, :, 1], 0))
    global_frame = frame_tile * tile_frames - margin + frame_pos
    global_row = row_tile * tile_rows - margin + row_pos
    own_frame = (frame_pos >= margin) & (frame_pos < margin + tile_frames)
    own_row = (row_pos >= margin) & (row_pos < margin + tile_rows)
    near_frame = (frame_pos >= margin - reach_frame) & (
        frame_pos < margin + tile_frames + reach_frame
    )
    near_frame = near_frame & (global_frame >= 0) & (global_frame < tiles_frames * tile_frames)
    near_row = (row_pos >= margin - reach_row) & (row_pos < margin + tile_rows + reach_row)
    near_row = near_row & (global_row >= 0) & (global_row < tiles_rows * tile_rows)
    onehot_frame = (
        jnp.floor_divide(global_frame, tile_frames)[:, None] == frame_ids[None, :]
    ).astype(jnp.float32)
    onehot_row = (jnp.floor_divide(global_row, tile_rows)[:, None] == row_ids[None, :]).astype(
        jnp.float32
    )
    valid = jnp.dot(jnp.dot(onehot_frame, tile_valid.astype(jnp.float32)), onehot_row.T) > 0.5
    allowed = (
        own_frame[:, None] & own_row[None, :] | near_frame[:, None] & near_row[None, :] & valid
    )
    return jnp.broadcast_to(allowed[:, :, None], (ext_frames, ext_rows, columns)).reshape(-1)


def attend(tile_queries, ext_keys, ext_values, d_mixed, allowed):
    score_scale = 1.0 / math.sqrt(HEAD_DIM)
    scores = (
        jnp.einsum("qhd,khd->hqk", tile_queries, ext_keys, preferred_element_type=jnp.float32)
        * score_scale
    )
    scores = jnp.where(allowed[None, None, :], scores, -1e30)
    row_max = jnp.max(scores, axis=-1, keepdims=True)
    expo = jnp.exp(scores - row_max)
    prob = expo / jnp.sum(expo, axis=-1, keepdims=True)
    probs = prob.astype(jnp.bfloat16)
    mixed = jnp.einsum(
        "hqk,khd->qhd", probs, ext_values, preferred_element_type=jnp.float32
    ).astype(jnp.bfloat16)
    d_probs = jnp.einsum("qhd,khd->hqk", d_mixed, ext_values, preferred_element_type=jnp.float32)
    inner = jnp.sum(prob * d_probs, axis=-1, keepdims=True)
    d_scores = (prob * (d_probs - inner) * score_scale).astype(jnp.bfloat16)
    d_query = jnp.einsum(
        "hqk,khd->qhd", d_scores, ext_keys, preferred_element_type=jnp.float32
    ).astype(jnp.bfloat16)
    d_key = jnp.einsum("hqk,qhd->khd", d_scores, tile_queries, preferred_element_type=jnp.float32)
    d_value = jnp.einsum("hqk,qhd->khd", probs, d_mixed, preferred_element_type=jnp.float32)
    return (mixed, d_query, d_key, d_value)


def shards(queries, key_tokens, value_tokens, out_weight, out_grad, window_reach, tile_valid):
    tile_frames, tile_rows, columns, width = queries.shape
    model_width = out_grad.shape[3]
    tokens = tile_frames * tile_rows * columns
    heads = width // HEAD_DIM
    margin = HALO
    ext_frames = tile_frames + 2 * margin
    ext_rows = tile_rows + 2 * margin
    ext_count = ext_frames * ext_rows * columns
    full_weight = lax.all_gather(out_weight, "height", axis=0, tiled=True)
    grad_rows = out_grad.reshape(tokens, model_width)
    d_mixed = lax.dot_general(
        grad_rows, full_weight, (((1,), (1,)), ((), ())), preferred_element_type=jnp.float32
    ).astype(jnp.bfloat16)
    stacked = jnp.stack([key_tokens, value_tokens], axis=3)
    extended = padded(stacked, (("tm", 0), ("height", 1)), margin)
    ext_keys = extended[:, :, :, 0, :].reshape(ext_count, heads, HEAD_DIM)
    ext_values = extended[:, :, :, 1, :].reshape(ext_count, heads, HEAD_DIM)
    frame_tile = lax.axis_index("tm")
    row_tile = lax.axis_index("height")
    allowed = key_mask(
        window_reach, tile_valid, frame_tile, row_tile, tile_frames, tile_rows, margin, columns
    )
    mixed, d_query, d_key, d_value = attend(
        queries.reshape(tokens, heads, HEAD_DIM),
        ext_keys,
        ext_values,
        d_mixed.reshape(tokens, heads, HEAD_DIM),
        allowed,
    )
    mixed_rows = mixed.reshape(tokens, width)
    attn_out = jnp.dot(mixed_rows, full_weight, preferred_element_type=jnp.float32).astype(
        jnp.bfloat16
    )
    attn_out = attn_out.reshape(tile_frames, tile_rows, columns, model_width)
    row_share = lax.psum_scatter(
        lax.dot_general(
            mixed_rows, grad_rows, (((0,), (0,)), ((), ())), preferred_element_type=jnp.float32
        ).astype(jnp.bfloat16),
        "height",
        scatter_dimension=0,
        tiled=True,
    )
    grad_weight = lax.psum_scatter(row_share, "tm", scatter_dimension=1, tiled=True).astype(
        jnp.float32
    )
    key_value_grads = jnp.stack(
        [d_key.reshape(ext_count, width), d_value.reshape(ext_count, width)], axis=1
    )
    key_value_grads = key_value_grads.reshape(ext_frames, ext_rows, columns, 2, width)
    upper_rows = key_value_grads[:, :margin]
    lower_rows = key_value_grads[:, margin + tile_rows :]
    middle_rows = key_value_grads[:, margin : margin + tile_rows]
    from_next_row = passed_along(upper_rows.astype(jnp.bfloat16), "height", -1).astype(
        upper_rows.dtype
    )
    from_prev_row = passed_along(lower_rows.astype(jnp.bfloat16), "height", 1).astype(
        lower_rows.dtype
    )
    middle_rows = jnp.concatenate(
        [
            middle_rows[:, :margin] + from_prev_row,
            middle_rows[:, margin : tile_rows - margin],
            middle_rows[:, tile_rows - margin :] + from_next_row,
        ],
        axis=1,
    )
    upper_frames = middle_rows[:margin]
    lower_frames = middle_rows[margin + tile_frames :]
    middle_frames = middle_rows[margin : margin + tile_frames]
    from_next_frame = passed_along(upper_frames.astype(jnp.bfloat16), "tm", -1).astype(
        upper_frames.dtype
    )
    from_prev_frame = passed_along(lower_frames.astype(jnp.bfloat16), "tm", 1).astype(
        lower_frames.dtype
    )
    own_grads = jnp.concatenate(
        [
            middle_frames[:margin] + from_prev_frame,
            middle_frames[margin : tile_frames - margin],
            middle_frames[tile_frames - margin :] + from_next_frame,
        ],
        axis=0,
    )
    grad_query = d_query.reshape(tile_frames, tile_rows, columns, width)
    grad_key = own_grads[:, :, :, 0, :].astype(jnp.bfloat16)
    grad_value = own_grads[:, :, :, 1, :].astype(jnp.bfloat16)
    return (attn_out, grad_query, grad_key, grad_value, grad_weight)


def solution(mesh):
    return jax.shard_map(
        shards,
        mesh=mesh,
        in_specs=(
            P("tm", "height", None, None),
            P("tm", "height", None, None),
            P("tm", "height", None, None),
            P("height", None),
            P("tm", "height", None, None),
            P(),
            P(),
        ),
        out_specs=(
            P("tm", "height", None, None),
            P("tm", "height", None, None),
            P("tm", "height", None, None),
            P("tm", "height", None, None),
            P("height", "tm"),
        ),
        check_vma=False,
    )
```

profile of v0, /device:TPU:0, one launch (start us, length us, event | category | flops | bytes accessed | tf_op | source)
XLA Modules:
  0.0 367.9 jit_solution(9377724077778961661)
XLA Ops:
  8.0 1.9 fusion.46
  9.9 1.3 collective-permute-start.1
  11.2 3.1 collective-permute-start
  14.3 1.1 reshape.126
  18.7 1.5 pad_maximum_fusion.5
  20.2 1.3 collective-permute-start.3
  21.5 6.3 %collective-permute-start.2 = (bf16[8,2,4,2,1536]{4,2,1,0,3:T(4,128)(2,1)}, bf16[8,2,4,2,1536]{4,2,1,0,3:T(4,128)(2,1)}, u32[]{:S(2)}, u32[]{:S(2)}) collective-permute-start(bf16[8,2,4,2,1536]{4,2,1,0,3:T(4,128)(2,1)} %get-tuple-element.22), channel_id=1, source_target_pairs={{0,1},{1,2},{2,3},{3,4},{4,5},{5,6},{6,7},{8,9},{9,10},{10,11},{11... | collective-permute-start | bytes 1179656 | tf_op jit(solution)/shard_map/ppermute | solution.py:18
  27.8 1.0 fusion.38
  29.2 14.2 %collective-permute-done.3 = bf16[8,2,4,2,1536]{4,2,1,0,3:T(4,128)(2,1)S(1)} collective-permute-done((bf16[8,2,4,2,1536]{4,2,1,0,3:T(4,128)(2,1)}, bf16[8,2,4,2,1536]{4,2,1,0,3:T(4,128)(2,1)S(1)}, u32[]{:S(2)}, u32[]{:S(2)}) %collective-permute-start.3) | collective-permute-done | bytes 393248 | tf_op jit(solution)/shard_map/ppermute | solution.py:19
  43.4 6.6 %collective-permute-done.2 = bf16[8,2,4,2,1536]{4,2,1,0,3:T(4,128)(2,1)} collective-permute-done((bf16[8,2,4,2,1536]{4,2,1,0,3:T(4,128)(2,1)}, bf16[8,2,4,2,1536]{4,2,1,0,3:T(4,128)(2,1)}, u32[]{:S(2)}, u32[]{:S(2)}) %collective-permute-start.2) | collective-permute-done | bytes 393248 | tf_op jit(solution)/shard_map/ppermute | solution.py:18
  50.0 3.2 pad_maximum_fusion.1
  53.1 0.9 fusion.65
  54.0 1.7 reshape_squeeze.6
  55.7 0.8 reshape_squeeze.7
  56.5 1.3 copy.35
  57.8 1.9 fusion.48
  59.8 0.8 fusion.68
  62.1 5.0 %convolution_convert_fusion = bf16[1536,3072]{1,0:T(8,128)(2,1)} fusion(bf16[128,1536]{0,1:T(8,128)(2,1)S(1)} %bitcast.51, bf16[128,3072]{1,0:T(8,128)(2,1)S(1)} %reshape.129), kind=kOutput, calls=%fused_computation.2 | convolution fusion | flops 1212678144 | bytes 10616832 | tf_op jit(solution)/shard_map/dot_general | solution.py:128
  67.3 91.7 %all-gather.2.cloned.1.call-done = bf16[1536,3072]{1,0:T(8,128)(2,1)} async-done(((bf16[192,3072]{1,0:T(8,128)(2,1)}), bf16[1536,3072]{1,0:T(8,128)(2,1)}) %all-gather.2.cloned.1.call-update) | async-done | bytes 9437200 | tf_op jit(solution)/shard_map/all_gather | solution.py:101
  159.0 6.9 %convolution_convert_fusion.2 = bf16[128,1536]{1,0:T(8,128)(2,1)S(1)} fusion(bf16[128,3072]{1,0:T(8,128)(2,1)S(1)} %reshape.129, bf16[1536,3072]{1,0:T(8,128)(2,1)} %all-gather.2.cloned.1.call-done), kind=kOutput, calls=%fused_computation.5 | convolution fusion | flops 1208156160 | bytes 10616832 | tf_op jit(solution)/shard_map/dot_general | solution.py:103
  166.2 1.9 fusion.42
  168.1 6.3 %fusion.15 = f32[384,12,128]{2,0,1:T(8,128)} fusion(f32[12,128,384]{1,2,0:T(8,128)} %fusion.42, bf16[128,12,128]{2,1,0:T(8,128)(2,1)S(1)} %copy-done.4, f32[12,128,384]{1,2,0:T(8,128)} %copy-done.9, f32[12,128]{1,0:T(8,128)S(1)} %get-tuple-element.30), kind=kOutput, calls=%fused_computation.18 | convolution fusion | flops 155125632 | bytes 7477248 | tf_op jit(solution)/shard_map/hqk,qhd->khd/dot_general | solution.py:87
  174.4 3.1 copy.39
  177.5 2.0 stack.19
  179.4 3.8 %convolution_bitcast_fusion = f32[384,12,128]{0,2,1:T(8,128)} fusion(bf16[128,12,128]{0,2,1:T(8,128)(2,1)} %bitcast.54, f32[12,128,384]{1,2,0:T(8,128)} %copy-done.9, f32[12,128]{1,0:T(8,128)S(1)} %get-tuple-element.30), kind=kOutput, calls=%fused_computation.17 | convolution fusion | flops 152174592 | bytes 5117952 | tf_op jit(solution)/shard_map/hqk,qhd->khd/dot_general | solution.py:88
  183.2 2.6 copy.41
  185.9 1.9 stack.20
  187.8 2.1 constant_dynamic-update-slice_fusion.1
  189.9 2.1 constant_dynamic-update-slice_fusion
  192.1 1.0 convert.12
  193.5 3.1 collective-permute-start.4
  196.6 1.3 collective-permute-start.5
  198.0 2.3 convolution_convert_fusion.1
  200.3 13.5 %collective-permute-done.4 = bf16[8,2,4,2,1536]{4,2,1,0,3:T(4,128)(2,1)S(1)} collective-permute-done((bf16[8,2,4,2,1536]{4,2,1,0,3:T(4,128)(2,1)S(1)}, bf16[8,2,4,2,1536]{4,2,1,0,3:T(4,128)(2,1)S(1)}, u32[]{:S(2)}, u32[]{:S(2)}) %collective-permute-start.4) | collective-permute-done | bytes 393248 | tf_op jit(solution)/shard_map/ppermute | solution.py:27
  213.8 2.4 collective-permute-done.5
  216.7 115.4 %reduce-scatter.3.cloned.1.call-done = bf16[192,3072]{1,0:T(8,128)(2,1)} async-done(((bf16[1536,3072]{1,0:T(8,128)(2,1)}), bf16[192,3072]{1,0:T(8,128)(2,1)}) %reduce-scatter.3.cloned.1.call-update) | async-done | bytes 1179664 | tf_op jit(solution)/shard_map/reduce_scatter | solution.py:127
  332.1 1.0 fusion.63
  333.1 1.2 fusion.66
  334.3 1.8 collective-permute-start.6
  336.1 1.5 collective-permute-start.7
  337.6 6.4 %fusion.21 = bf16[128,12,128]{0,2,1:T(8,128)(2,1)} fusion(bf16[384,12,128]{0,2,1:T(8,128)(2,1)} %copy-done.1, f32[12,128,384]{1,2,0:T(8,128)} %fusion.42, f32[12,128,384]{1,2,0:T(8,128)} %copy-done.9, f32[12,128]{1,0:T(8,128)S(1)} %get-tuple-element.30), kind=kOutput, calls=%fused_computation.22 | convolution fusion | flops 155322240 | bytes 6297600 | tf_op jit(solution)/shard_map/hqk,khd->qhd/dot_general | solution.py:84
  344.0 2.4 reshape.128
  346.4 2.2 copy.37
  348.5 2.0 reshape.131
  351.3 1.5 slice_add_fusion.1
  353.3 1.2 slice_bitcast_fusion
  354.5 5.0 %reduce-scatter.5.cloned.1.call-done = bf16[192,768]{1,0:T(8,128)(2,1)} async-done(((bf16[192,3072]{1,0:T(8,128)(2,1)}), bf16[192,768]{1,0:T(8,128)(2,1)}) %reduce-scatter.5.cloned.1.call-update) | async-done | bytes 294928 | tf_op jit(solution)/shard_map/reduce_scatter | solution.py:135
  359.5 1.8 convert_element_type.75
  (55 shorter events, 6.0 us)
Async XLA Ops:
  7.2 11.5 %copy-start.2 = (bf16[4,8,4,1536]{3,2,1,0:T(4,128)(2,1)S(1)}, bf16[4,8,4,1536]{3,2,1,0:T(4,128)(2,1)}, u32[]{:S(2)}) copy-start(bf16[4,8,4,1536]{3,2,1,0:T(4,128)(2,1)} %param.8) | copy-start | bytes 1179652
  7.2 11.5 %copy-start.3 = (bf16[4,8,4,1536]{3,2,1,0:T(4,128)(2,1)S(1)}, bf16[4,8,4,1536]{3,2,1,0:T(4,128)(2,1)}, u32[]{:S(2)}) copy-start(bf16[4,8,4,1536]{3,2,1,0:T(4,128)(2,1)} %param.9) | copy-start | bytes 1179652
  7.2 7.1 %copy-start.8 = (s32[4,8,2]{1,2,0:T(2,128)S(1)}, s32[4,8,2]{1,2,0:T(2,128)}, u32[]{:S(2)}) copy-start(s32[4,8,2]{1,2,0:T(2,128)} %param.12) | copy-start | bytes 772
  7.2 7.1 %copy-start.7 = (bf16[4,8,4,1536]{3,2,1,0:T(4,128)(2,1)S(1)}, bf16[4,8,4,1536]{3,2,1,0:T(4,128)(2,1)}, u32[]{:S(2)}) copy-start(bf16[4,8,4,1536]{3,2,1,0:T(4,128)(2,1)} %param.7) | copy-start | bytes 1179652
  7.2 151.8 %all-gather.2.cloned.1.call-start = ((), (), s32[]{:S(2)}) async-start(), calls=%async_computation.2 | async-start | bytes 10616832 | tf_op jit(solution)/shard_map/all_gather | solution.py:101
  7.9 324.2 %reduce-scatter.3.cloned.1.call-start = ((), (), s32[]{:S(2)}) async-start(), calls=%async_computation.3 | async-start | bytes 10616832 | tf_op jit(solution)/shard_map/reduce_scatter | solution.py:127
  8.0 21.0 %copy-start.6 = (bf16[4,8,4,3072]{3,2,1,0:T(4,128)(2,1)S(1)}, bf16[4,8,4,3072]{3,2,1,0:T(4,128)(2,1)}, u32[]{:S(2)}) copy-start(bf16[4,8,4,3072]{3,2,1,0:T(4,128)(2,1)} %param.11) | copy-start | bytes 2359300
  9.9 8.8 %collective-permute-start.1 = (bf16[2,8,4,2,1536]{4,2,1,0,3:T(4,128)(2,1)S(1)}, bf16[2,8,4,2,1536]{4,2,1,0,3:T(4,128)(2,1)S(1)}, u32[]{:S(2)}, u32[]{:S(2)}) collective-permute-start(bf16[2,8,4,2,1536]{4,2,1,0,3:T(4,128)(2,1)S(1)} %get-tuple-element.27), channel_id=1, source_target_pairs={{8,0},{16,8},{24,16},{9,1},{17,9},{25,17},{10,2},{18,10},{26,18},{... | collective-permute-start | bytes 1179656 | tf_op jit(solution)/shard_map/ppermute | solution.py:19
  11.2 7.5 %collective-permute-start = (bf16[2,8,4,2,1536]{4,2,1,0,3:T(4,128)(2,1)S(1)}, bf16[2,8,4,2,1536]{4,2,1,0,3:T(4,128)(2,1)S(1)}, u32[]{:S(2)}, u32[]{:S(2)}) collective-permute-start(bf16[2,8,4,2,1536]{4,2,1,0,3:T(4,128)(2,1)S(1)} %get-tuple-element.26), channel_id=1, source_target_pairs={{0,8},{8,16},{16,24},{1,9},{9,17},{17,25},{2,10},{10,18},{18,26},{... | collective-permute-start | bytes 1179656 | tf_op jit(solution)/shard_map/ppermute | solution.py:18
  20.2 23.2 %collective-permute-start.3 = (bf16[8,2,4,2,1536]{4,2,1,0,3:T(4,128)(2,1)}, bf16[8,2,4,2,1536]{4,2,1,0,3:T(4,128)(2,1)S(1)}, u32[]{:S(2)}, u32[]{:S(2)}) collective-permute-start(bf16[8,2,4,2,1536]{4,2,1,0,3:T(4,128)(2,1)} %get-tuple-element.23), channel_id=1, source_target_pairs={{1,0},{2,1},{3,2},{4,3},{5,4},{6,5},{7,6},{9,8},{10,9},{11,10},{12... | collective-permute-start | bytes 1179656 | tf_op jit(solution)/shard_map/ppermute | solution.py:19
  21.5 28.5 %collective-permute-start.2 = (bf16[8,2,4,2,1536]{4,2,1,0,3:T(4,128)(2,1)}, bf16[8,2,4,2,1536]{4,2,1,0,3:T(4,128)(2,1)}, u32[]{:S(2)}, u32[]{:S(2)}) collective-permute-start(bf16[8,2,4,2,1536]{4,2,1,0,3:T(4,128)(2,1)} %get-tuple-element.22), channel_id=1, source_target_pairs={{0,1},{1,2},{2,3},{3,4},{4,5},{5,6},{6,7},{8,9},{9,10},{10,11},{11... | collective-permute-start | bytes 1179656 | tf_op jit(solution)/shard_map/ppermute | solution.py:18
  57.8 2.8 copy-start.1
  59.8 1.4 copy-start
  60.7 1.4 copy-start.9
  67.1 292.4 %reduce-scatter.5.cloned.1.call-start = ((), (), s32[]{:S(2)}) async-start(), calls=%async_computation.4 | async-start | bytes 1474560 | tf_op jit(solution)/shard_map/reduce_scatter | solution.py:135
  165.9 2.2 copy-start.4
  166.2 1.9 copy-start.5
  187.8 10.2 %slice-start = ((s8[9437184]{0:T(1024)(128)(4,1)}), s8[4194304]{0:T(1024)(128)(4,1)S(1)}, s32[]{:S(2)}) async-start(s8[9437184]{0:T(1024)(128)(4,1)} %bitcast.43), calls=%async_computation.5 | async-start | bytes 8388608
  189.9 8.0 %slice-start.1 = ((s8[9437184]{0:T(1024)(128)(4,1)}), s8[4194304]{0:T(1024)(128)(4,1)S(1)}, s32[]{:S(2)}) async-start(s8[9437184]{0:T(1024)(128)(4,1)} %bitcast.43), calls=%async_computation.6 | async-start | bytes 8388608
  192.0 5.9 %slice-start.2 = ((s8[9437184]{0:T(1024)(128)(4,1)}), s8[1048576]{0:T(1024)(128)(4,1)S(1)}, s32[]{:S(2)}) async-start(s8[9437184]{0:T(1024)(128)(4,1)} %bitcast.43), calls=%async_computation.7 | async-start | bytes 2097152
  193.5 20.3 %collective-permute-start.4 = (bf16[8,2,4,2,1536]{4,2,1,0,3:T(4,128)(2,1)S(1)}, bf16[8,2,4,2,1536]{4,2,1,0,3:T(4,128)(2,1)S(1)}, u32[]{:S(2)}, u32[]{:S(2)}) collective-permute-start(bf16[8,2,4,2,1536]{4,2,1,0,3:T(4,128)(2,1)S(1)} %get-tuple-element.16), channel_id=1, source_target_pairs={{0,1},{1,2},{2,3},{3,4},{4,5},{5,6},{6,7},{8,9},{9,10},{10,11},{11... | collective-permute-start | bytes 1179656 | tf_op jit(solution)/shard_map/ppermute | solution.py:27
  196.6 19.6 %collective-permute-start.5 = (bf16[8,2,4,2,1536]{4,2,1,0,3:T(4,128)(2,1)S(1)}, bf16[8,2,4,2,1536]{4,2,1,0,3:T(4,128)(2,1)S(1)}, u32[]{:S(2)}, u32[]{:S(2)}) collective-permute-start(bf16[8,2,4,2,1536]{4,2,1,0,3:T(4,128)(2,1)S(1)} %get-tuple-element.17), channel_id=1, source_target_pairs={{1,0},{2,1},{3,2},{4,3},{5,4},{6,5},{7,6},{9,8},{10,9},{11,10},{12... | collective-permute-start | bytes 1179656 | tf_op jit(solution)/shard_map/ppermute | solution.py:27
  334.3 17.0 %collective-permute-start.6 = (bf16[2,8,4,2,1536]{4,2,1,0,3:T(4,128)(2,1)}, bf16[2,8,4,2,1536]{4,2,1,0,3:T(4,128)(2,1)S(1)}, u32[]{:S(2)}, u32[]{:S(2)}) collective-permute-start(bf16[2,8,4,2,1536]{4,2,1,0,3:T(4,128)(2,1)} %get-tuple-element.20), channel_id=1, source_target_pairs={{0,8},{8,16},{16,24},{1,9},{9,17},{17,25},{2,10},{10,18},{18,26},{... | collective-permute-start | bytes 1179656 | tf_op jit(solution)/shard_map/ppermute | solution.py:27
  336.1 15.2 %collective-permute-start.7 = (bf16[2,8,4,2,1536]{4,2,1,0,3:T(4,128)(2,1)}, bf16[2,8,4,2,1536]{4,2,1,0,3:T(4,128)(2,1)}, u32[]{:S(2)}, u32[]{:S(2)}) collective-permute-start(bf16[2,8,4,2,1536]{4,2,1,0,3:T(4,128)(2,1)} %get-tuple-element.21), channel_id=1, source_target_pairs={{8,0},{16,8},{24,16},{9,1},{17,9},{25,17},{10,2},{18,10},{26,18},{... | collective-permute-start | bytes 1179656 | tf_op jit(solution)/shard_map/ppermute | solution.py:27
Sparse Core Ops, SparseCore 0:
  10.2 148.7 all-gather.1
  162.6 169.4 reduce-scatter.2
  334.7 24.8 reduce-scatter.4
where the time goes:
time: 369 us; the launch traced here: 368 us
  waiting for transfers between devices  250 us (68%)
  matrix products  36.3 us (10%)
  local copies, waits for them, and re-layouts  30.1 us (8%)
  starting transfers between devices  19.9 us (5%)
  between operations  16.8 us (5%)
  other arithmetic  15.2 us (4%)
    reduce_scatter x1, waiting for transfers between devices, shards(): lax.psum_scatter(lax.dot_general(mixed_rows, grad_rows, (((0,), (0,)), ((...  115 us
    all_gather x1, waiting for transfers between devices, shards(): full_weight = lax.all_gather(out_weight, 'height', axis=0, tiled=True)  91.7 us
    ppermute x4, waiting for transfers between devices, passed_along(): lax.ppermute(value, axis, [(source, source + steps) for source in range(f...  15.9 us
    ppermute x2, waiting for transfers between devices, padded(): after = lax.ppermute(first, axis, down)  14.2 us
    ppermute x2, starting transfers between devices, padded(): before = lax.ppermute(last, axis, up)  9.32 us
    ppermute x4, starting transfers between devices, passed_along(): lax.ppermute(value, axis, [(source, source + steps) for source in range(f...  7.74 us
  transfers between devices with their start and end apart: 11, of which 7 were waited for; matrix products, arithmetic and copies ran while one was open for 21% of the time, Pallas kernels for 0%

commit v1 on v0

--- a/solution.py
+++ b/solution.py
@@ -6,6 +6,20 @@
 
 HEAD_DIM = 128
 HALO = 2
+
+
+def store_modes(buf):
+    degree = lax.axis_size("height")
+    vals = list(map(lambda i0: (i0, (i0 + 1) % degree), range(degree)))
+
+    def wait_terms(z2):
+        if len(z2) == degree:
+            return z2
+        return wait_terms([lax.ppermute(z2[0], axis_name="height", perm=vals), *z2])
+
+    return jnp.roll(
+        jnp.concatenate(wait_terms([buf]), 0), (lax.axis_index("height") + 1) * buf.shape[0], 0
+    )
 
 
 def padded(shard, sides, width):
@@ -98,7 +112,7 @@
     ext_frames = tile_frames + 2 * margin
     ext_rows = tile_rows + 2 * margin
     ext_count = ext_frames * ext_rows * columns
-    full_weight = lax.all_gather(out_weight, "height", axis=0, tiled=True)
+    full_weight = store_modes(out_weight)
     grad_rows = out_grad.reshape(tokens, model_width)
     d_mixed = lax.dot_general(
         grad_rows, full_weight, (((1,), (1,)), ((), ())), preferred_element_type=jnp.float32

time: 369 us -> 448 us (1.21)
  waiting for transfers between devices: 250 us -> 303 us
  local copies, waits for them, and re-layouts: 30.1 us -> 53.5 us
    ppermute x0 -> x7, waiting for transfers between devices: none -> 274 us  [wait_terms(): return wait_terms([lax.ppermute(z2[0], axis_name='height', perm=vals), *z2])]
    reduce_scatter x1, waiting for transfers between devices: 115 us -> 9.47 us  [shards(): lax.psum_scatter(lax.dot_general(mixed_rows, grad_rows, (((0,), (0,)), ((...]
    all_gather x1 -> x0, waiting for transfers between devices: 91.7 us -> none  [shards(): full_weight = lax.all_gather(out_weight, 'height', axis=0, tiled=True)]
    unnamed x27 -> x62, local copies, waits for them, and re-layouts: 2.8 us -> 22.3 us
    ppermute x4, waiting for transfers between devices: 15.9 us -> 0.41 us  [passed_along(): lax.ppermute(value, axis, [(source, source + steps) for source in range(f...]
    ppermute x2, waiting for transfers between devices: 14.2 us -> 0.01 us  [padded(): after = lax.ppermute(first, axis, down)]
    ppermute x0 -> x7, starting transfers between devices: none -> 8.34 us  [wait_terms(): return wait_terms([lax.ppermute(z2[0], axis_name='height', perm=vals), *z2])]
    dot_general x1, matrix products: 2.33 us -> 7.6 us  [shards(): jnp.dot(mixed_rows, full_weight, preferred_element_type=jnp.float32)]
  transfers between devices with their start and end apart: 11 -> 17, of which waited for: 7 -> 11; matrix products, arithmetic and copies ran while one was open for 21% -> 15% of each run, Pallas kernels for 0% -> 0%
where the time goes in v1:
time: 448 us; the launch traced here: 447 us
  waiting for transfers between devices  303 us (68%)
  local copies, waits for them, and re-layouts  53.5 us (12%)
  matrix products  34.2 us (8%)
  starting transfers between devices  23.2 us (5%)
  between operations  17.2 us (4%)
  other arithmetic  16.1 us (4%)
    ppermute x7, waiting for transfers between devices, wait_terms(): return wait_terms([lax.ppermute(z2[0], axis_name='height', perm=vals), *z2])  274 us
    unnamed x62, local copies, waits for them, and re-layouts  22.3 us
    ppermute x2, waiting for transfers between devices, padded(): before = lax.ppermute(last, axis, up)  10.1 us
    reduce_scatter x1, waiting for transfers between devices, shards(): lax.psum_scatter(lax.dot_general(mixed_rows, grad_rows, (((0,), (0,)), ((...  9.47 us
  transfers between devices with their start and end apart: 17, of which 11 were waited for; matrix products, arithmetic and copies ran while one was open for 15% of the time, Pallas kernels for 0%

profile of v1, /device:TPU:0, one launch (start us, length us, event | category | flops | bytes accessed | tf_op | source)
XLA Modules:
  0.0 446.8 jit_solution(12593749229126414763)
XLA Ops:
  7.2 1.9 fusion.56
  9.1 2.5 collective-permute-start
  13.7 1.6 reshape.129
  19.2 1.4 pad_maximum_fusion.5
  20.6 4.3 collective-permute-start.2
  26.7 1.6 fusion.48
  30.7 10.0 %collective-permute-done.2 = bf16[8,2,4,2,1536]{4,2,1,0,3:T(4,128)(2,1)S(1)} collective-permute-done((bf16[8,2,4,2,1536]{4,2,1,0,3:T(4,128)(2,1)}, bf16[8,2,4,2,1536]{4,2,1,0,3:T(4,128)(2,1)S(1)}, u32[]{:S(2)}, u32[]{:S(2)}) %collective-permute-start.2) | collective-permute-done | bytes 393248 | tf_op jit(solution)/shard_map/ppermute | solution.py:32
  40.8 3.2 pad_maximum_fusion.1
  43.9 2.1 fusion.77
  48.1 3.1 reshape_squeeze.6
  51.2 2.0 fusion.58
  55.6 5.0 %convolution_convert_fusion = bf16[1536,3072]{1,0:T(8,128)(2,1)} fusion(bf16[128,1536]{0,1:T(8,128)(2,1)S(1)} %bitcast.49, bf16[128,3072]{1,0:T(8,128)(2,1)S(1)} %reshape.129), kind=kOutput, calls=%fused_computation.2 | convolution fusion | flops 1212678144 | bytes 10616832 | tf_op jit(solution)/shard_map/dot_general | solution.py:142
  61.9 2.4 collective-permute-start.4
  64.3 48.3 %collective-permute-done.4 = bf16[192,3072]{1,0:T(8,128)(2,1)S(1)} collective-permute-done((bf16[192,3072]{1,0:T(8,128)(2,1)S(1)}, bf16[192,3072]{1,0:T(8,128)(2,1)S(1)}, u32[]{:S(2)}, u32[]{:S(2)}) %collective-permute-start.4) | collective-permute-done | bytes 1179680 | tf_op jit(solution)/shard_map/ppermute | solution.py:18
  112.5 2.9 collective-permute-start.5
  115.4 53.5 %collective-permute-done.5 = bf16[192,3072]{1,0:T(8,128)(2,1)S(1)} collective-permute-done((bf16[192,3072]{1,0:T(8,128)(2,1)S(1)}, bf16[192,3072]{1,0:T(8,128)(2,1)S(1)}, u32[]{:S(2)}, u32[]{:S(2)}) %collective-permute-start.5) | collective-permute-done | bytes 1179680 | tf_op jit(solution)/shard_map/ppermute | solution.py:18
  169.5 52.1 %collective-permute-done.6 = bf16[192,3072]{1,0:T(8,128)(2,1)S(1)} collective-permute-done((bf16[192,3072]{1,0:T(8,128)(2,1)S(1)}, bf16[192,3072]{1,0:T(8,128)(2,1)S(1)}, u32[]{:S(2)}, u32[]{:S(2)}) %collective-permute-start.6) | collective-permute-done | bytes 1179680 | tf_op jit(solution)/shard_map/ppermute | solution.py:18
  222.6 37.5 %collective-permute-done.7 = bf16[192,3072]{1,0:T(8,128)(2,1)S(1)} collective-permute-done((bf16[192,3072]{1,0:T(8,128)(2,1)S(1)}, bf16[192,3072]{1,0:T(8,128)(2,1)S(1)}, u32[]{:S(2)}, u32[]{:S(2)}) %collective-permute-start.7) | collective-permute-done | bytes 1179680 | tf_op jit(solution)/shard_map/ppermute | solution.py:18
  261.1 2.5 collective-permute-start.8
  263.6 26.7 %collective-permute-done.8 = bf16[192,3072]{1,0:T(8,128)(2,1)S(1)} collective-permute-done((bf16[192,3072]{1,0:T(8,128)(2,1)S(1)}, bf16[192,3072]{1,0:T(8,128)(2,1)S(1)}, u32[]{:S(2)}, u32[]{:S(2)}) %collective-permute-start.8) | collective-permute-done | bytes 1179680 | tf_op jit(solution)/shard_map/ppermute | solution.py:18
  291.3 28.3 %collective-permute-done.9 = bf16[192,3072]{1,0:T(8,128)(2,1)} collective-permute-done((bf16[192,3072]{1,0:T(8,128)(2,1)S(1)}, bf16[192,3072]{1,0:T(8,128)(2,1)}, u32[]{:S(2)}, u32[]{:S(2)}) %collective-permute-start.9) | collective-permute-done | bytes 1179680 | tf_op jit(solution)/shard_map/ppermute | solution.py:18
  319.6 27.6 %collective-permute-done.10 = bf16[192,3072]{1,0:T(8,128)(2,1)} collective-permute-done((bf16[192,3072]{1,0:T(8,128)(2,1)}, bf16[192,3072]{1,0:T(8,128)(2,1)}, u32[]{:S(2)}, u32[]{:S(2)}) %collective-permute-start.10) | collective-permute-done | bytes 1179680 | tf_op jit(solution)/shard_map/ppermute | solution.py:18
  347.2 1.3 constant_dynamic-update-slice_fusion.15
  348.5 1.4 constant_dynamic-update-slice_fusion.14
  351.6 1.3 constant_dynamic-update-slice_fusion.7
  353.0 1.3 constant_dynamic-update-slice_fusion.6
  355.8 2.7 fusion.9
  358.5 5.1 %copy-done.1 = bf16[3072,3072]{1,0:T(8,128)(2,1)} copy-done((bf16[3072,3072]{1,0:T(8,128)(2,1)}, bf16[3072,3072]{1,0:T(8,128)(2,1)S(1)}, u32[]{:S(2)}) %copy-start.1) | copy-done | bytes 18874392
  363.6 2.0 convolution_bitcast_fusion
  365.6 2.6 copy.39
  368.3 1.9 stack.20
  370.1 1.9 fusion.52
  372.1 1.4 copy-done.15
  373.5 4.8 %fusion.25 = f32[384,12,128]{2,0,1:T(8,128)} fusion(f32[12,128,384]{1,2,0:T(8,128)S(1)} %fusion.52, bf16[128,12,128]{2,1,0:T(8,128)(2,1)S(1)} %copy-done.18, f32[12,128,384]{1,2,0:T(8,128)} %copy-done.21, f32[12,128]{1,0:T(8,128)S(1)} %get-tuple-element.30), kind=kOutput, calls=%fused_computation.22 | convolution fusion | flops 155125632 | bytes 7477248 | tf_op jit(solution)/shard_map/hqk,qhd->khd/dot_general | solution.py:101
  378.3 3.2 copy.37
  381.4 1.9 stack.19
  383.3 2.1 constant_dynamic-update-slice_fusion.17
  388.6 1.5 collective-permute-start.12
  390.3 7.6 %fusion.6 = bf16[128,3072]{1,0:T(8,128)(2,1)} fusion(bf16[128,1536]{0,1:T(8,128)(2,1)S(1)} %bitcast.50, bf16[3072,3072]{1,0:T(8,128)(2,1)} %copy-done.1, s32[]{:T(128)S(6)} %select_n.52), kind=kOutput, calls=%fused_computation.7 | convolution fusion | flops 1208352768 | bytes 10616836 | tf_op jit(solution)/shard_map/dot_general | solution.py:137
  398.7 9.5 %reduce-scatter.3.cloned.1.call-done = bf16[192,3072]{1,0:T(8,128)(2,1)} async-done(((bf16[1536,3072]{1,0:T(8,128)(2,1)}), bf16[192,3072]{1,0:T(8,128)(2,1)}) %reduce-scatter.3.cloned.1.call-update) | async-done | bytes 1179664 | tf_op jit(solution)/shard_map/reduce_scatter | solution.py:141
  410.4 1.4 collective-permute-start.13
  413.1 5.9 %fusion.31 = bf16[128,12,128]{0,2,1:T(8,128)(2,1)} fusion(bf16[384,12,128]{0,2,1:T(8,128)(2,1)} %copy-done.10, f32[12,128,384]{1,2,0:T(8,128)} %copy-done.15, f32[12,128,384]{1,2,0:T(8,128)} %copy-done.21, f32[12,128]{1,0:T(8,128)S(1)} %get-tuple-element.30), kind=kOutput, calls=%fused_computation.26 | convolution fusion | flops 155322240 | bytes 6297600 | tf_op jit(solution)/shard_map/hqk,khd->qhd/dot_general | solution.py:98
  418.9 2.2 copy.35
  421.1 2.0 reshape.131
  423.1 2.4 reshape.128
  426.3 1.5 slice_add_fusion.1
  429.5 8.7 %reduce-scatter.5.cloned.1.call-done = bf16[192,768]{1,0:T(8,128)(2,1)} async-done(((bf16[192,3072]{1,0:T(8,128)(2,1)}), bf16[192,768]{1,0:T(8,128)(2,1)}) %reduce-scatter.5.cloned.1.call-update) | async-done | bytes 294928 | tf_op jit(solution)/shard_map/reduce_scatter | solution.py:149
  438.2 1.8 convert_element_type.79
  (100 shorter events, 30.2 us)
Async XLA Ops:
  7.2 12.1 %copy-start.11 = (bf16[4,8,4,1536]{3,2,1,0:T(4,128)(2,1)S(1)}, bf16[4,8,4,1536]{3,2,1,0:T(4,128)(2,1)}, u32[]{:S(2)}) copy-start(bf16[4,8,4,1536]{3,2,1,0:T(4,128)(2,1)} %param.8) | copy-start | bytes 1179652
  7.2 12.1 %copy-start.12 = (bf16[4,8,4,1536]{3,2,1,0:T(4,128)(2,1)S(1)}, bf16[4,8,4,1536]{3,2,1,0:T(4,128)(2,1)}, u32[]{:S(2)}) copy-start(bf16[4,8,4,1536]{3,2,1,0:T(4,128)(2,1)} %param.9) | copy-start | bytes 1179652
  7.2 401.0 %reduce-scatter.3.cloned.1.call-start = ((), (), s32[]{:S(2)}) async-start(), calls=%async_computation.2 | async-start | bytes 10616832 | tf_op jit(solution)/shard_map/reduce_scatter | solution.py:141
  9.1 20.6 %copy-start.19 = (bf16[4,8,4,1536]{3,2,1,0:T(4,128)(2,1)S(1)}, bf16[4,8,4,1536]{3,2,1,0:T(4,128)(2,1)}, u32[]{:S(2)}) copy-start(bf16[4,8,4,1536]{3,2,1,0:T(4,128)(2,1)} %param.7) | copy-start | bytes 1179652
  9.1 10.1 %collective-permute-start = (bf16[2,8,4,2,1536]{4,2,1,0,3:T(4,128)(2,1)S(1)}, bf16[2,8,4,2,1536]{4,2,1,0,3:T(4,128)(2,1)S(1)}, u32[]{:S(2)}, u32[]{:S(2)}) collective-permute-start(bf16[2,8,4,2,1536]{4,2,1,0,3:T(4,128)(2,1)S(1)} %get-tuple-element.26), channel_id=1, source_target_pairs={{0,8},{8,16},{16,24},{1,9},{9,17},{17,25},{2,10},{10,18},{18,26},{... | collective-permute-start | bytes 1179656 | tf_op jit(solution)/shard_map/ppermute | solution.py:32
  11.6 7.6 %collective-permute-start.1 = (bf16[2,8,4,2,1536]{4,2,1,0,3:T(4,128)(2,1)S(1)}, bf16[2,8,4,2,1536]{4,2,1,0,3:T(4,128)(2,1)S(1)}, u32[]{:S(2)}, u32[]{:S(2)}) collective-permute-start(bf16[2,8,4,2,1536]{4,2,1,0,3:T(4,128)(2,1)S(1)} %get-tuple-element.27), channel_id=1, source_target_pairs={{8,0},{16,8},{24,16},{9,1},{17,9},{25,17},{10,2},{18,10},{26,18},{... | collective-permute-start | bytes 1179656 | tf_op jit(solution)/shard_map/ppermute | solution.py:33
  15.3 40.3 %copy-start.13 = (bf16[128,3072]{1,0:T(8,128)(2,1)}, bf16[128,3072]{1,0:T(8,128)(2,1)S(1)}, u32[]{:S(2)}) copy-start(bf16[128,3072]{1,0:T(8,128)(2,1)S(1)} %reshape.129) | copy-start | bytes 2359300
  20.6 20.2 %collective-permute-start.2 = (bf16[8,2,4,2,1536]{4,2,1,0,3:T(4,128)(2,1)}, bf16[8,2,4,2,1536]{4,2,1,0,3:T(4,128)(2,1)S(1)}, u32[]{:S(2)}, u32[]{:S(2)}) collective-permute-start(bf16[8,2,4,2,1536]{4,2,1,0,3:T(4,128)(2,1)} %get-tuple-element.22), channel_id=1, source_target_pairs={{0,1},{1,2},{2,3},{3,4},{4,5},{5,6},{6,7},{8,9},{9,10},{10,11},{11... | collective-permute-start | bytes 1179656 | tf_op jit(solution)/shard_map/ppermute | solution.py:32
  24.9 15.9 %collective-permute-start.3 = (bf16[8,2,4,2,1536]{4,2,1,0,3:T(4,128)(2,1)S(1)}, bf16[8,2,4,2,1536]{4,2,1,0,3:T(4,128)(2,1)}, u32[]{:S(2)}, u32[]{:S(2)}) collective-permute-start(bf16[8,2,4,2,1536]{4,2,1,0,3:T(4,128)(2,1)S(1)} %get-tuple-element.23), channel_id=1, source_target_pairs={{1,0},{2,1},{3,2},{4,3},{5,4},{6,5},{7,6},{9,8},{10,9},{11,10},{12... | collective-permute-start | bytes 1179656 | tf_op jit(solution)/shard_map/ppermute | solution.py:33
  48.1 5.1 %copy-start.10 = (bf16[384,12,128]{0,2,1:T(8,128)(2,1)}, bf16[384,12,128]{0,2,1:T(8,128)(2,1)S(1)}, u32[]{:S(2)}) copy-start(bf16[384,12,128]{0,2,1:T(8,128)(2,1)S(1)} %copy.33) | copy-start | bytes 3538948
  51.2 2.9 copy-start.2
  51.2 2.0 copy-start.20
  54.1 1.5 copy-start.21
  55.6 5.1 %copy-start.16 = (bf16[12,128,128]{2,1,0:T(8,128)(2,1)}, bf16[12,128,128]{2,1,0:T(8,128)(2,1)S(1)}, u32[]{:S(2)}) copy-start(bf16[12,128,128]{2,1,0:T(8,128)(2,1)S(1)} %convolution_convert_fusion.1) | copy-start | bytes 1179652
  60.6 1.3 copy-start.3
  60.6 377.5 %reduce-scatter.5.cloned.1.call-start = ((), (), s32[]{:S(2)}) async-start(), calls=%async_computation.3 | async-start | bytes 1474560 | tf_op jit(solution)/shard_map/reduce_scatter | solution.py:149
  61.9 50.6 %collective-permute-start.4 = (bf16[192,3072]{1,0:T(8,128)(2,1)S(1)}, bf16[192,3072]{1,0:T(8,128)(2,1)S(1)}, u32[]{:S(2)}, u32[]{:S(2)}) collective-permute-start(bf16[192,3072]{1,0:T(8,128)(2,1)S(1)} %copy-done.3), channel_id=1, source_target_pairs={{0,1},{1,2},{2,3},{3,4},{4,5},{5,6},{6,7},{7,0},{8,9},{9,10},{10,1... | collective-permute-start | bytes 3538952 | tf_op jit(solution)/shard_map/ppermute | solution.py:18
  112.5 56.4 %collective-permute-start.5 = (bf16[192,3072]{1,0:T(8,128)(2,1)S(1)}, bf16[192,3072]{1,0:T(8,128)(2,1)S(1)}, u32[]{:S(2)}, u32[]{:S(2)}) collective-permute-start(bf16[192,3072]{1,0:T(8,128)(2,1)S(1)} %collective-permute-done.4), channel_id=1, source_target_pairs={{0,1},{1,2},{2,3},{3,4},{4,5},{5,6},{6,7},{7,0},{8,9},{9,10},{10,1... | collective-permute-start | bytes 3538952 | tf_op jit(solution)/shard_map/ppermute | solution.py:18
  168.9 52.6 %collective-permute-start.6 = (bf16[192,3072]{1,0:T(8,128)(2,1)S(1)}, bf16[192,3072]{1,0:T(8,128)(2,1)S(1)}, u32[]{:S(2)}, u32[]{:S(2)}) collective-permute-start(bf16[192,3072]{1,0:T(8,128)(2,1)S(1)} %collective-permute-done.5), channel_id=1, source_target_pairs={{0,1},{1,2},{2,3},{3,4},{4,5},{5,6},{6,7},{7,0},{8,9},{9,10},{10,1... | collective-permute-start | bytes 3538952 | tf_op jit(solution)/shard_map/ppermute | solution.py:18
  221.6 1.0 copy-start.4
  222.6 37.5 %collective-permute-start.7 = (bf16[192,3072]{1,0:T(8,128)(2,1)S(1)}, bf16[192,3072]{1,0:T(8,128)(2,1)S(1)}, u32[]{:S(2)}, u32[]{:S(2)}) collective-permute-start(bf16[192,3072]{1,0:T(8,128)(2,1)S(1)} %collective-permute-done.6), channel_id=1, source_target_pairs={{0,1},{1,2},{2,3},{3,4},{4,5},{5,6},{6,7},{7,0},{8,9},{9,10},{10,1... | collective-permute-start | bytes 3538952 | tf_op jit(solution)/shard_map/ppermute | solution.py:18
  260.1 1.0 copy-start.6
  261.1 29.2 %collective-permute-start.8 = (bf16[192,3072]{1,0:T(8,128)(2,1)S(1)}, bf16[192,3072]{1,0:T(8,128)(2,1)S(1)}, u32[]{:S(2)}, u32[]{:S(2)}) collective-permute-start(bf16[192,3072]{1,0:T(8,128)(2,1)S(1)} %collective-permute-done.7), channel_id=1, source_target_pairs={{0,1},{1,2},{2,3},{3,4},{4,5},{5,6},{6,7},{7,0},{8,9},{9,10},{10,1... | collective-permute-start | bytes 3538952 | tf_op jit(solution)/shard_map/ppermute | solution.py:18
  290.3 1.0 copy-start.8
  291.3 28.3 %collective-permute-start.9 = (bf16[192,3072]{1,0:T(8,128)(2,1)S(1)}, bf16[192,3072]{1,0:T(8,128)(2,1)}, u32[]{:S(2)}, u32[]{:S(2)}) collective-permute-start(bf16[192,3072]{1,0:T(8,128)(2,1)S(1)} %collective-permute-done.8), channel_id=1, source_target_pairs={{0,1},{1,2},{2,3},{3,4},{4,5},{5,6},{6,7},{7,0},{8,9},{9,10},{10,1... | collective-permute-start | bytes 3538952 | tf_op jit(solution)/shard_map/ppermute | solution.py:18
  319.6 27.6 %collective-permute-start.10 = (bf16[192,3072]{1,0:T(8,128)(2,1)}, bf16[192,3072]{1,0:T(8,128)(2,1)}, u32[]{:S(2)}, u32[]{:S(2)}) collective-permute-start(bf16[192,3072]{1,0:T(8,128)(2,1)} %collective-permute-done.9), channel_id=1, source_target_pairs={{0,1},{1,2},{2,3},{3,4},{4,5},{5,6},{6,7},{7,0},{8,9},{9,10},{10,1... | collective-permute-start | bytes 3538952 | tf_op jit(solution)/shard_map/ppermute | solution.py:18
  319.6 30.4 %copy-start.9 = (bf16[192,3072]{1,0:T(8,128)(2,1)S(1)}, bf16[192,3072]{1,0:T(8,128)(2,1)}, u32[]{:S(2)}) copy-start(bf16[192,3072]{1,0:T(8,128)(2,1)} %copy-done.8) | copy-start | bytes 3538948
  348.5 1.6 copy-start.7
  350.0 1.3 copy-start.5
  354.7 1.1 copy-start.14
  355.8 7.8 %copy-start.1 = (bf16[3072,3072]{1,0:T(8,128)(2,1)}, bf16[3072,3072]{1,0:T(8,128)(2,1)S(1)}, u32[]{:S(2)}) copy-start(bf16[3072,3072]{1,0:T(8,128)(2,1)S(1)} %constant_dynamic-update-slice_fusion) | copy-start | bytes 56623108
  355.8 7.8 %copy-start.22 = (f32[12,128,384]{1,2,0:T(8,128)S(1)}, f32[12,128,384]{1,2,0:T(8,128)}, u32[]{:S(2)}) copy-start(f32[12,128,384]{1,2,0:T(8,128)} %copy-done.21) | copy-start | bytes 7077892
  370.1 3.3 copy-start.18
  372.1 1.4 copy-start.15
  383.3 2.4 copy-start
  387.0 3.3 copy-start.17
  387.3 10.6 %collective-permute-start.11 = (bf16[8,2,4,2,1536]{4,2,1,0,3:T(4,128)(2,1)S(1)}, bf16[8,2,4,2,1536]{4,2,1,0,3:T(4,128)(2,1)S(1)}, u32[]{:S(2)}, u32[]{:S(2)}) collective-permute-start(bf16[8,2,4,2,1536]{4,2,1,0,3:T(4,128)(2,1)S(1)} %get-tuple-element.16), channel_id=1, source_target_pairs={{0,1},{1,2},{2,3},{3,4},{4,5},{5,6},{6,7},{8,9},{9,10},{10,11},{11... | collective-permute-start | bytes 1179656 | tf_op jit(solution)/shard_map/ppermute | solution.py:41
  388.6 9.7 %collective-permute-start.12 = (bf16[8,2,4,2,1536]{4,2,1,0,3:T(4,128)(2,1)S(1)}, bf16[8,2,4,2,1536]{4,2,1,0,3:T(4,128)(2,1)S(1)}, u32[]{:S(2)}, u32[]{:S(2)}) collective-permute-start(bf16[8,2,4,2,1536]{4,2,1,0,3:T(4,128)(2,1)S(1)} %get-tuple-element.17), channel_id=1, source_target_pairs={{1,0},{2,1},{3,2},{4,3},{5,4},{6,5},{7,6},{9,8},{10,9},{11,10},{12... | collective-permute-start | bytes 1179656 | tf_op jit(solution)/shard_map/ppermute | solution.py:41
  410.4 15.9 %collective-permute-start.13 = (bf16[2,8,4,2,1536]{4,2,1,0,3:T(4,128)(2,1)}, bf16[2,8,4,2,1536]{4,2,1,0,3:T(4,128)(2,1)S(1)}, u32[]{:S(2)}, u32[]{:S(2)}) collective-permute-start(bf16[2,8,4,2,1536]{4,2,1,0,3:T(4,128)(2,1)} %get-tuple-element.20), channel_id=1, source_target_pairs={{0,8},{8,16},{16,24},{1,9},{9,17},{17,25},{2,10},{10,18},{18,26},{... | collective-permute-start | bytes 1179656 | tf_op jit(solution)/shard_map/ppermute | solution.py:41
  411.8 14.5 %collective-permute-start.14 = (bf16[2,8,4,2,1536]{4,2,1,0,3:T(4,128)(2,1)}, bf16[2,8,4,2,1536]{4,2,1,0,3:T(4,128)(2,1)}, u32[]{:S(2)}, u32[]{:S(2)}) collective-permute-start(bf16[2,8,4,2,1536]{4,2,1,0,3:T(4,128)(2,1)} %get-tuple-element.21), channel_id=1, source_target_pairs={{8,0},{16,8},{24,16},{9,1},{17,9},{25,17},{10,2},{18,10},{26,18},{... | collective-permute-start | bytes 1179656 | tf_op jit(solution)/shard_map/ppermute | solution.py:41
Sparse Core Ops, SparseCore 0:
  60.8 347.4 reduce-scatter.2
  410.8 27.3 reduce-scatter.4
